TPU v7x, 32 devices: a whole 2x2x4 slice. The times are simulated.
32 devices in a mesh: group: 2 (over y), context: 4 (over z), head: 4 (over x, core).
Axes of the slice: x: 2, y: 2, z: 4, core: 2. Of those that a mesh axis runs over, the one named last changes fastest.
Arguments:
- dn_query: bfloat16 [1024, 2048], P(('group', 'context'), 'head'), parts along dimension 0, may hold values from -6 to 6
- dn_key: bfloat16 [1024, 2048], P(('group', 'context'), 'head'), parts along dimension 0, may hold values from -6 to 6
- dn_value: bfloat16 [1024, 4096], P(('group', 'context'), 'head'), parts along dimension 0, may hold values from -6 to 6
- dn_gate: bfloat16 [1024, 4096], P(('group', 'context'), 'head'), parts along dimension 0, may hold values from -6 to 6
- dn_beta_logit: float32 [1024, 32], P(('group', 'context'), 'head'), parts along dimension 0, may hold values from -6 to 6
- dn_decay: float32 [1024, 32], P(('group', 'context'), 'head'), parts along dimension 0, may hold values from -1 to 0
- dn_norm_gain: float32 [128], replicated, may hold values from 0.1 to 1.9
- prefix_state: bfloat16 [4, 32, 128, 128], P('group', 'head', 'context'), parts along dimension 0, may hold values from -6 to 6
- at_query: bfloat16 [1024, 4096], P(('group', 'context'), 'head'), parts along dimension 0, may hold values from -6 to 6
- at_gate: bfloat16 [1024, 4096], P(('group', 'context'), 'head'), parts along dimension 0, may hold values from -6 to 6
- at_key: bfloat16 [1024, 512], P(('group', 'context')), parts along dimension 0, may hold values from -6 to 6
- at_value: bfloat16 [1024, 512], P(('group', 'context')), parts along dimension 0, may hold values from -6 to 6
- prefix_key: bfloat16 [16, 64, 512], P(('group', 'context')), parts along dimension 0, may hold values from -6 to 6
- prefix_value: bfloat16 [16, 64, 512], P(('group', 'context')), parts along dimension 0, may hold values from -6 to 6
- req_len: int32 [8], P('group'), parts along dimension 0, may hold values from 1 to 256, 512 in all
- req_prefix: int32 [8], P('group'), parts along dimension 0, may hold values from 0 to 1, as said below
- req_offset: int32 [8], P('group'), parts along dimension 0, may hold values from 64 to 256, as said below
- block_table: int32 [16], P('group'), parts along dimension 0, may hold values from 0 to 7, each once
Outputs:
- dn_out: bfloat16 [1024, 4096], P(('group', 'context'), 'head'), parts along dimension 0
- at_out: bfloat16 [1024, 4096], P(('group', 'context'), 'head'), parts along dimension 0
There are 2 independent parts, one for each index of `group`. A program takes and returns all parts, laid end to end along the dimension named above; an argument that names none is the same for every part. Nothing has to cross between parts.
Inputs may be any that keep to these rules, and one draw needn't show every extreme that they name: `req_len`: requests lie one after another in row order; the longest has exactly 256 new tokens. `req_prefix`: every prefix is extended by one or more requests. `req_offset`: equal for the requests of one prefix: the number of its cached positions; one prefix holds 256, another from a quarter to a half of 256. `block_table`: entry p * 4 + j is the slot of block j of prefix p; every slot once.
All inputs are finite; a program needn't handle non-finite values.
Results may differ from a plain program's by a relative error of at most 0.011.
Values may be sent and summed in bfloat16 or wider, within the bound.
A program may use at most 128 MiB of HBM per device.

v0:
```python
import math
import jax
import jax.numpy as jnp
from jax import lax
from jax.sharding import PartitionSpec as P

VH = 32
KH = 16
DK = 128
DV = 128
HQ = 16
KVH = 2
HD = 256
ROT = 64
ROPE_THETA = 10000000.0
YARN_FACTOR = 4.0
YARN_ANCHOR = 262144.0
NEG_LARGE = -1e30
HIGH = lax.Precision.HIGHEST


def carried_in(x, axis, join, neutral):
    place = lax.axis_index(axis)
    gathered = jax.tree.map(
        lambda a, kind: lax.all_gather(a.astype(kind), axis),
        x,
        (jnp.bfloat16, jnp.bfloat16, jnp.bfloat16),
    )
    state = jax.tree.map(lambda a, e: jnp.zeros_like(a) + jnp.asarray(e, a.dtype), x, neutral)

    def one(turn, state):
        return join(
            state,
            jax.tree.map(
                lambda a, own: lax.dynamic_index_in_dim(a, turn, 0, False).astype(own.dtype),
                gathered,
                x,
            ),
        )

    return lax.fori_loop(0, place, one, state)


def yarn_tables(positions, rotary):
    half = rotary // 2
    log_theta = math.log(ROPE_THETA)
    lower = max(
        math.floor(rotary * math.log(YARN_ANCHOR / (64.0 * math.pi)) / (2.0 * log_theta)), 0
    )
    upper = min(
        math.ceil(rotary * math.log(YARN_ANCHOR / (2.0 * math.pi)) / (2.0 * log_theta)), rotary - 1
    )
    spread = float(upper - lower)
    index = jnp.arange(half, dtype=jnp.float32)
    plain_frequency = jnp.exp(index * (-2.0 * log_theta / rotary))
    keep = 1.0 - jnp.clip((index - lower) / spread, 0.0, 1.0)
    frequency = plain_frequency * keep + plain_frequency / YARN_FACTOR * (1.0 - keep)
    angles = positions.astype(jnp.float32)[:, None] * frequency[None, :]
    attention_factor = 0.1 * math.log(YARN_FACTOR) + 1.0
    return (jnp.cos(angles) * attention_factor, jnp.sin(angles) * attention_factor)


def rotate(values, cosines, sines, rotary):
    half = rotary // 2
    first = values[..., :half]
    second = values[..., half:rotary]
    cosines = cosines[:, None, :]
    sines = sines[:, None, :]
    return jnp.concatenate(
        [first * cosines - second * sines, second * cosines + first * sines, values[..., rotary:]],
        axis=-1,
    )


def unit_rows(values):
    return values * lax.rsqrt(jnp.sum(values * values, axis=-1, keepdims=True) + 1e-06)


def row_layout(rows, req_len, req_prefix, req_offset):
    starts = jnp.cumsum(req_len) - req_len
    leading_found = (starts[None, :] <= rows[:, None]).astype(jnp.int32)
    segment = jnp.sum(leading_found, axis=1) - 1
    choose = (segment[:, None] == jnp.arange(req_len.shape[0], dtype=jnp.int32)[None, :]).astype(
        jnp.int32
    )
    first = jnp.sum(choose * starts[None, :], axis=1)
    prefix = jnp.sum(choose * req_prefix[None, :], axis=1)
    offset = jnp.sum(choose * req_offset[None, :], axis=1)
    return (segment, first, prefix, offset, offset + rows - first)


def absorb(state, queries, search_handles, values, visible):
    peak, total, summed = state
    scores = jnp.einsum(
        "thd,nd->thn", queries, search_handles, preferred_element_type=jnp.float32
    ) * search_handles.shape[-1] ** (-0.5)
    seen = visible[:, None, :]
    scores = jnp.where(seen, scores, NEG_LARGE)
    new_peak = jnp.maximum(peak, jnp.max(scores, axis=-1))
    weights = jnp.where(seen, jnp.exp(scores - new_peak[..., None]), 0.0)
    shrink = jnp.exp(peak - new_peak)
    total = total * shrink + jnp.sum(weights, axis=-1)
    summed = summed * shrink[..., None] + jnp.einsum(
        "thn,nd->thd", weights.astype(jnp.bfloat16), values, preferred_element_type=jnp.float32
    )
    return (new_peak, total, summed)


def compose(earlier, later):
    map_early, add_early, flag_early = earlier
    map_late, add_late, flag_late = later
    fresh = flag_late > 0.5
    joined_map = jnp.where(
        fresh, map_late, jnp.einsum("hij,hjk->hik", map_early, map_late, precision=HIGH)
    )
    joined_add = jnp.where(
        fresh, add_late, jnp.einsum("hvj,hjk->hvk", add_early, map_late, precision=HIGH) + add_late
    )
    return (joined_map, joined_add, jnp.maximum(flag_early, flag_late))


def shards(
    dn_query,
    dn_key,
    dn_value,
    dn_gate,
    dn_beta_logit,
    dn_decay,
    dn_norm_gain,
    prefix_state,
    at_query,
    at_gate,
    at_key,
    at_value,
    prefix_key,
    prefix_value,
    req_len,
    req_prefix,
    req_offset,
    block_table,
):
    tokens_here = dn_query.shape[0]
    key_heads = dn_query.shape[1] // DK
    value_heads = dn_value.shape[1] // DV
    query_heads = at_query.shape[1] // HD
    device = lax.axis_index("context")
    row_start = device * tokens_here
    rows = row_start + jnp.arange(tokens_here, dtype=jnp.int32)
    segment, first, prefix, offset, position = row_layout(rows, req_len, req_prefix, req_offset)
    query = jnp.repeat(
        unit_rows(dn_query.reshape(tokens_here, key_heads, DK).astype(jnp.float32)) * DK ** (-0.5),
        VH // KH,
        axis=1,
    )
    key = jnp.repeat(
        unit_rows(dn_key.reshape(tokens_here, key_heads, DK).astype(jnp.float32)), VH // KH, axis=1
    )
    query_heads_first = jnp.transpose(query, (1, 0, 2))
    key_heads_first = jnp.transpose(key, (1, 0, 2))
    value_heads_first = jnp.transpose(
        dn_value.reshape(tokens_here, value_heads, DV).astype(jnp.float32), (1, 0, 2)
    )
    beta = jax.nn.sigmoid(dn_beta_logit).T
    same = segment[:, None] == segment[None, :]
    causal = same & (rows[:, None] >= rows[None, :])
    strict = same & (rows[:, None] > rows[None, :])
    running = jnp.dot(causal.astype(jnp.float32), dn_decay, precision=HIGH).T
    gaps = running[:, :, None] - running[:, None, :]
    decay_mat = jnp.where(causal[None], jnp.exp(jnp.where(causal[None], gaps, 0.0)), 0.0)
    key_gram = jnp.einsum("hid,hjd->hij", key_heads_first, key_heads_first, precision=HIGH)
    query_key = jnp.einsum("hid,hjd->hij", query_heads_first, key_heads_first, precision=HIGH)
    lower_mat = jnp.where(strict[None], beta[:, :, None] * key_gram * decay_mat, 0.0)
    system = jnp.eye(tokens_here, dtype=jnp.float32)[None] + lower_mat
    start_decay = jnp.exp(running)
    solve_values = beta[:, :, None] * value_heads_first
    solve_keys = (beta * start_decay)[:, :, None] * key_heads_first
    solved = jax.scipy.linalg.solve_triangular(
        system, jnp.concatenate([solve_values, solve_keys], axis=2), lower=True, unit_diagonal=True
    )
    update = solved[:, :, :DV]
    wy_keys = solved[:, :, DV:]
    mixing = decay_mat * query_key
    local_out = jnp.einsum("hij,hjv->hiv", mixing, update, precision=HIGH)
    reach = start_decay[:, :, None] * query_heads_first - jnp.einsum(
        "hij,hjk->hik", mixing, wy_keys, precision=HIGH
    )
    tail = segment == segment[tokens_here - 1]
    end_gaps = running[:, tokens_here - 1 : tokens_here] - running
    end_weight = jnp.where(tail[None, :], jnp.exp(jnp.where(tail[None, :], end_gaps, 0.0)), 0.0)
    end_decay = start_decay[:, tokens_here - 1]
    identity_mat = jnp.eye(DK, dtype=jnp.float32)
    carry_map = end_decay[:, None, None] * identity_mat[None] - jnp.einsum(
        "hjk,hj,hjl->hkl", wy_keys, end_weight, key_heads_first, precision=HIGH
    )
    carry_add = jnp.einsum("hjv,hj,hjl->hvl", update, end_weight, key_heads_first, precision=HIGH)
    restart = (first[tokens_here - 1] >= row_start).astype(jnp.float32)
    identity = (
        jnp.broadcast_to(identity_mat, (value_heads, DK, DK)),
        jnp.zeros((value_heads, DV, DK), jnp.float32),
        jnp.zeros((), jnp.float32),
    )
    into_map, into_add, into_flag = carried_in(
        (carry_map, carry_add, restart), "context", compose, identity
    )
    carried = ((segment == segment[0]) & (first[0] < row_start))[None, :, None]
    through = jnp.einsum("hkl,hil->hik", into_map, reach, precision=HIGH)
    extra = jnp.einsum("hvk,hik->hiv", into_add, reach, precision=HIGH)
    weight_vec = jnp.where(carried, through, reach).astype(jnp.bfloat16)
    core = local_out + jnp.where(carried, extra, 0.0)
    owner_ids = jnp.arange(prefix_state.shape[0], dtype=jnp.int32)
    select = (prefix[None, :] == owner_ids[:, None]).astype(jnp.bfloat16)
    masked = select[:, None, :, None] * weight_vec[None]
    state_part = jnp.einsum(
        "phik,phvk->hiv",
        masked,
        lax.all_gather(prefix_state, "context", axis=2, tiled=True),
        preferred_element_type=jnp.float32,
    )
    core = core + state_part
    core_rows = jnp.transpose(core, (1, 0, 2))
    normed = core_rows * lax.rsqrt(jnp.mean(core_rows * core_rows, axis=-1, keepdims=True) + 1e-06)
    gate_rows = dn_gate.reshape(tokens_here, value_heads, DV).astype(jnp.float32)
    dn_out = (
        (normed * dn_norm_gain * jax.nn.silu(gate_rows))
        .reshape(tokens_here, value_heads * DV)
        .astype(jnp.bfloat16)
    )
    group = HQ // KVH
    kv_head = lax.axis_index("head") * query_heads // group
    cosines, sines = yarn_tables(position, ROT)
    query_rot = rotate(
        at_query.reshape(tokens_here, query_heads, HD).astype(jnp.float32), cosines, sines, ROT
    ).astype(jnp.bfloat16)
    new_key = lax.dynamic_slice_in_dim(at_key, kv_head * HD, HD, 1).reshape(tokens_here, 1, HD)
    new_key = (
        rotate(new_key.astype(jnp.float32), cosines, sines, ROT)
        .reshape(tokens_here, HD)
        .astype(jnp.bfloat16)
    )
    new_value = lax.dynamic_slice_in_dim(at_value, kv_head * HD, HD, 1)
    cached_key = lax.dynamic_slice_in_dim(prefix_key, kv_head * HD, HD, 2)
    cached_value = lax.dynamic_slice_in_dim(prefix_value, kv_head * HD, HD, 2)
    table_index = jnp.arange(block_table.shape[0], dtype=jnp.int32)
    blocks_per_prefix = block_table.shape[0] // prefix_state.shape[0]
    state = (
        jnp.full((tokens_here, query_heads), NEG_LARGE, jnp.float32),
        jnp.zeros((tokens_here, query_heads), jnp.float32),
        jnp.zeros((tokens_here, query_heads, HD), jnp.float32),
    )
    search_handles = lax.all_gather(cached_key, "context", axis=0, tiled=True)
    values = lax.all_gather(cached_value, "context", axis=0, tiled=True)
    count = search_handles.shape[0]
    width = search_handles.shape[1]
    slots = jnp.arange(count, dtype=jnp.int32)
    entry = jnp.sum(
        jnp.where(block_table[None, :] == slots[:, None], table_index[None, :], 0), axis=1
    )
    owner = jnp.repeat(entry // blocks_per_prefix, width)
    where_in = (
        (entry % blocks_per_prefix)[:, None] * width + jnp.arange(width, dtype=jnp.int32)[None, :]
    ).reshape(count * width)
    visible = (owner[None, :] == prefix[:, None]) & (where_in[None, :] < offset[:, None])
    flat_keys = search_handles.reshape(count * width, search_handles.shape[2])
    flat_values = values.reshape(count * width, values.shape[2])
    state = absorb(state, query_rot, flat_keys, flat_values, visible)
    search_handles = lax.all_gather(new_key, "context", axis=0, tiled=True)
    values = lax.all_gather(new_value, "context", axis=0, tiled=True)
    key_rows = jnp.arange(search_handles.shape[0], dtype=jnp.int32)
    key_segment = row_layout(key_rows, req_len, req_prefix, req_offset)[0]
    visible = (key_segment[None, :] == segment[:, None]) & (key_rows[None, :] <= rows[:, None])
    state = absorb(state, query_rot, search_handles, values, visible)
    peak, total, summed = state
    attention = summed / total[..., None]
    gate_att = at_gate.reshape(tokens_here, query_heads, HD).astype(jnp.float32)
    at_out = (
        (attention * jax.nn.sigmoid(gate_att))
        .reshape(tokens_here, query_heads * HD)
        .astype(jnp.bfloat16)
    )
    return (dn_out, at_out)


def solution(mesh):
    placed = (
        P(("group", "context"), "head"),
        P(("group", "context"), "head"),
        P(("group", "context"), "head"),
        P(("group", "context"), "head"),
        P(("group", "context"), "head"),
        P(("group", "context"), "head"),
        P(),
        P("group", "head", "context", None),
        P(("group", "context"), "head"),
        P(("group", "context"), "head"),
        P(("group", "context"), None),
        P(("group", "context"), None),
        P(("group", "context"), None, None),
        P(("group", "context"), None, None),
        P("group"),
        P("group"),
        P("group"),
        P("group"),
    )
    return jax.shard_map(
        shards,
        mesh=mesh,
        in_specs=placed,
        out_specs=(P(("group", "context"), "head"), P(("group", "context"), "head")),
        check_vma=False,
    )
```

profile of v0, /device:TPU:26, one launch (start us, length us, event | category | flops | bytes accessed | tf_op | source)
XLA Modules:
  0.0 243.3 jit_solution(15976261732324481945)
XLA Ops:
  12.8 2.1 fusion.15
  14.9 79.4 %custom-call.4 = f32[8,1,128,128]{2,3,1,0:T(8,128)S(1)} custom-call(f32[8,1,128,128]{3,2,1,0:T(8,128)} %fusion.15), custom_call_target="InvertDiagBlocksLowerTriangular" | custom-call | tf_op jit(solution)/shard_map/jit(_solve_triangular)/vmap()/triangular_solve | solution.py:177
  94.3 1.8 compare_and_fusion.3
  96.7 1.0 fusion.22
  97.8 1.7 convolution_convert_fusion
  99.8 1.7 fusion.20
  104.2 16.7 %all-gather.2 = bf16[512,1,256]{0,2,1:T(8,128)(2,1)} all-gather(bf16[128,1,256]{0,2,1:T(8,128)(2,1)S(1)} %pad_maximum_fusion.1), channel_id=4, replica_groups=mesh['group'=2,'context'=4,'head'=4] {'context'}, dimensions={0}, use_global_device_ids=true | all-gather | bytes 327680 | tf_op jit(solution)/shard_map/all_gather | solution.py:266
  121.9 16.6 %all_gather.40 = bf16[8,64,256]{2,1,0:T(8,128)(2,1)} all-gather(bf16[2,64,256]{2,1,0:T(8,128)(2,1)S(1)} %constant_dynamic-slice_fusion.3), channel_id=1, replica_groups=mesh['group'=2,'context'=4,'head'=4] {'context'}, dimensions={0}, use_global_device_ids=true | all-gather | bytes 327680 | tf_op jit(solution)/shard_map/all_gather | solution.py:250
  138.9 16.8 %all_gather.41 = bf16[8,64,256]{2,1,0:T(8,128)(2,1)} all-gather(bf16[2,64,256]{2,1,0:T(8,128)(2,1)S(1)} %constant_dynamic-slice_fusion.2), channel_id=1, replica_groups=mesh['group'=2,'context'=4,'head'=4] {'context'}, dimensions={0}, use_global_device_ids=true | all-gather | bytes 327680 | tf_op jit(solution)/shard_map/all_gather | solution.py:251
  155.7 16.5 %all_gather.43 = bf16[512,256]{1,0:T(8,128)(2,1)} all-gather(bf16[128,256]{1,0:T(8,128)(2,1)S(1)} %constant_dynamic-slice_fusion.4), channel_id=1, replica_groups=mesh['group'=2,'context'=4,'head'=4] {'context'}, dimensions={0}, use_global_device_ids=true | all-gather | bytes 327680 | tf_op jit(solution)/shard_map/all_gather | solution.py:267
  172.5 1.0 copy.164
  180.1 1.2 fusion.18
  181.8 1.9 dynamic-update-slice
  183.7 2.3 fusion.19
  186.6 8.6 %all-reduce = bf16[4]{0:T(256)(128)(2,1)} all-reduce(bf16[4]{0:T(256)(128)(2,1)S(1)} %copy-done.39), channel_id=1, replica_groups=mesh['group'=2,'context'=4,'head'=4] {'context'}, use_global_device_ids=true, to_apply=%add | all-reduce | flops 4 | bytes 16
  195.3 1.1 copy.165
  198.4 0.9 copy-done.13
  199.7 15.1 %all_gather.39 = bf16[2,8,128,128]{3,2,0,1:T(8,128)(2,1)S(1)} all-gather(bf16[2,8,32,128]{3,2,0,1:T(8,128)(2,1)S(1)} %copy.150), channel_id=1, replica_groups=mesh['group'=2,'context'=4,'head'=4] {'context'}, dimensions={2}, use_global_device_ids=true | all-gather | bytes 655360 | tf_op jit(solution)/shard_map/all_gather | solution.py:216
  216.1 1.2 convolution_multiply_fusion.3
  217.3 1.5 fusion.43
  220.2 11.2 %while.14 = (s32[]{:T(128)}, f32[8,128,128]{1,2,0:T(8,128)S(1)}, f32[8,128,128]{1,2,0:T(8,128)S(1)}, s32[]{:T(128)}, bf16[4]{0:T(256)(128)(2,1)S(1)}, /*index=5*...) while((s32[]{:T(128)}, f32[8,128,128]{1,2,0:T(8,128)S(1)}, ...), condition=%wide.region_6.7_spmd, body=%wide.region_5.6_spmd.sunk | while | flops 403308544 | bytes 7340196 | solution.py:41
  220.2 1.1 constant_dynamic-slice_fusion.7
  223.9 1.1 constant_dynamic-slice_fusion.7
  227.7 1.1 constant_dynamic-slice_fusion.7
  (191 shorter events, 32.6 us)
Async XLA Ops:
  7.2 96.5 %copy-start = (bf16[128,512]{1,0:T(8,128)(2,1)S(1)}, bf16[128,512]{1,0:T(8,128)(2,1)}, u32[]{:S(2)}) copy-start(bf16[128,512]{1,0:T(8,128)(2,1)} %param.30) | copy-start | bytes 393220
  7.2 212.3 %all-gather.8.cloned.1.call-start = ((), (), s32[]{:S(2)}) async-start(), calls=%async_computation.1 | async-start | bytes 1310720 | tf_op jit(solution)/shard_map/all_gather | solution.py:25
  7.2 3.6 %copy-start.15 = (bf16[128,512]{1,0:T(8,128)(2,1)S(1)}, bf16[128,512]{1,0:T(8,128)(2,1)}, u32[]{:S(2)}) copy-start(bf16[128,512]{1,0:T(8,128)(2,1)} %param.21) | copy-start | bytes 393220
  7.3 92.5 %copy-start.2 = (f32[128,128]{1,0:T(8,128)}, f32[128,128]{1,0:T(8,128)S(1)}, u32[]{:S(2)}) copy-start(f32[128,128]{1,0:T(8,128)S(1)} %get-tuple-element.158) | copy-start | bytes 196612
  9.0 166.3 %copy-start.28 = (s32[128]{0:T(128)}, s32[128]{0:T(128)S(1)}, u32[]{:S(2)}) copy-start(s32[128]{0:T(128)S(1)} %get-tuple-element.108) | copy-start | bytes 1540
  9.0 1.3 copy-start.34
  10.6 85.6 %copy-start.18 = (f32[8,128]{1,0:T(8,128)}, f32[8,128]{1,0:T(8,128)S(1)}, u32[]{:S(2)}) copy-start(f32[8,128]{1,0:T(8,128)S(1)} %convolution_bitcast_fusion.3) | copy-start | bytes 12292
  11.4 1.0 copy-start.10
  96.2 3.4 %copy-start.20 = (f32[8,128]{1,0:T(8,128)}, f32[8,128]{1,0:T(8,128)S(1)}, u32[]{:S(2)}) copy-start(f32[8,128]{1,0:T(8,128)S(1)} %get-tuple-element.135) | copy-start | bytes 12292
  99.5 120.0 %all-gather.6.cloned.1.call-start = ((), (), s32[]{:S(2)}) async-start(), calls=%async_computation | async-start | bytes 1310720 | tf_op jit(solution)/shard_map/all_gather | solution.py:25
  120.9 1.0 copy-start.22
  121.9 16.6 %copy-start.36 = (s32[8]{0:T(128)S(1)}, s32[8]{0:T(128)}, u32[]{:S(2)}) copy-start(s32[8]{0:T(128)} %param.37) | copy-start | bytes 100
  121.9 17.0 %copy-start.23 = (bf16[2,64,512]{2,1,0:T(8,128)(2,1)S(1)}, bf16[2,64,512]{2,1,0:T(8,128)(2,1)}, u32[]{:S(2)}) copy-start(bf16[2,64,512]{2,1,0:T(8,128)(2,1)} %param.33) | copy-start | bytes 393220
  138.9 16.8 %copy-start.24 = (bf16[128,512]{1,0:T(8,128)(2,1)S(1)}, bf16[128,512]{1,0:T(8,128)(2,1)}, u32[]{:S(2)}) copy-start(bf16[128,512]{1,0:T(8,128)(2,1)} %param.31) | copy-start | bytes 393220
  155.7 16.5 %copy-start.12 = (bf16[128,1024]{1,0:T(8,128)(2,1)S(1)}, bf16[128,1024]{1,0:T(8,128)(2,1)}, u32[]{:S(2)}) copy-start(bf16[128,1024]{1,0:T(8,128)(2,1)} %param.29) | copy-start | bytes 786436
  172.5 1.0 copy-start.16
  175.2 1.0 copy-start.14
  178.2 1.9 copy-start.6
  180.1 3.6 %copy-start.4 = (f32[128,4,256]{2,0,1:T(8,128)S(1)}, f32[128,4,256]{2,0,1:T(8,128)}, u32[]{:S(2)}) copy-start(f32[128,4,256]{2,0,1:T(8,128)} %copy.164) | copy-start | bytes 1572868
  183.7 2.3 copy-start.9
  186.0 9.2 %copy-start.3 = (f32[128,128]{1,0:T(8,128)S(1)}, f32[128,128]{1,0:T(8,128)}, u32[]{:S(2)}) copy-start(f32[128,128]{1,0:T(8,128)} %copy-done.2) | copy-start | bytes 196612
  199.7 15.2 %copy-start.29 = (s32[128]{0:T(128)S(1)}, s32[128]{0:T(128)}, u32[]{:S(2)}) copy-start(s32[128]{0:T(128)} %copy-done.28) | copy-start | bytes 1540
  217.3 1.5 copy-start.21
  232.7 1.0 copy-start.1
  (18 other events, 13.3 us)
Sparse Core Ops, SparseCore 0:
  99.7 32.8 all-gather.7
  134.7 33.2 all-gather.5
where the time goes:
time: 244 us; the launch traced here: 243 us
  blocking collectives  90.3 us (37%)
  other arithmetic  87.6 us (36%)
  local copies, waits for them, and re-layouts  27.8 us (11%)
  matrix products  19.2 us (8%)
  between operations  16.1 us (7%)
    another operation x2, other arithmetic, shards(): jax.scipy.linalg.solve_triangular(system, jnp.concatenate([solve_values,...  79.4 us
    all_gather x1, blocking collectives, shards(): values = lax.all_gather(cached_value, 'context', axis=0, tiled=True)  16.8 us
    all_gather x1, blocking collectives, shards(): search_handles = lax.all_gather(new_key, 'context', axis=0, tiled=True)  16.7 us
    all_gather x1, blocking collectives, shards(): search_handles = lax.all_gather(cached_key, 'context', axis=0, tiled=True)  16.6 us
    all_gather x1, blocking collectives, shards(): values = lax.all_gather(new_value, 'context', axis=0, tiled=True)  16.5 us
    unnamed x91, local copies, waits for them, and re-layouts  15.3 us
    all_gather x1, blocking collectives, shards(): lax.all_gather(prefix_state, 'context', axis=2, tiled=True)  15.1 us
    unnamed x1, blocking collectives  8.58 us
  transfers between devices with their start and end apart: 2, of which 0 were waited for; matrix products, arithmetic and copies ran while one was open for 9% of the time, Pallas kernels for 0%

commit v1 on v0

--- a/solution.py
+++ b/solution.py
@@ -264,7 +264,14 @@
     flat_values = values.reshape(count * width, values.shape[2])
     state = absorb(state, query_rot, flat_keys, flat_values, visible)
     search_handles = lax.all_gather(new_key, "context", axis=0, tiled=True)
-    values = lax.all_gather(new_value, "context", axis=0, tiled=True)
+    ring = [new_value]
+    for hop in range(3):
+        ring.append(lax.ppermute(ring[-1], "context", [(dev, (dev + 1) % 4) for dev in range(4)]))
+    values = jnp.roll(
+        jnp.concatenate(ring[::-1], axis=0),
+        (lax.axis_index("context") + 1) * ring[0].shape[0],
+        axis=0,
+    )
     key_rows = jnp.arange(search_handles.shape[0], dtype=jnp.int32)
     key_segment = row_layout(key_rows, req_len, req_prefix, req_offset)[0]
     visible = (key_segment[None, :] == segment[:, None]) & (key_rows[None, :] <= rows[:, None])

time: 244 us -> 227 us (0.930)
  blocking collectives: 90.3 us -> 71.1 us
  starting transfers between devices: 0.08 us -> 6.16 us
  other arithmetic: 87.6 us -> 84.5 us
    all_gather x1 -> x0, blocking collectives: 16.5 us -> none  [shards(): values = lax.all_gather(new_value, 'context', axis=0, tiled=True)]
    ppermute x0 -> x3, starting transfers between devices: none -> 6.08 us  [shards(): lax.ppermute(ring[-1], 'context', [(dev, (dev + 1) % 4) for dev in range(...]
    unnamed x91 -> x76, local copies, waits for them, and re-layouts: 15.3 us -> 16.9 us
  transfers between devices with their start and end apart: 2 -> 5, of which waited for: 0 -> 0; matrix products, arithmetic and copies ran while one was open for 9% -> 10% of each run, Pallas kernels for 0% -> 0%
where the time goes in v1:
time: 227 us; the launch traced here: 226 us
  other arithmetic  84.5 us (37%)
  blocking collectives  71.1 us (31%)
  local copies, waits for them, and re-layouts  28.5 us (13%)
  matrix products  17.1 us (8%)
  between operations  16 us (7%)
  starting transfers between devices  6.16 us (3%)
    another operation x2, other arithmetic, shards(): jax.scipy.linalg.solve_triangular(system, jnp.concatenate([solve_values,...  78.6 us
    all_gather x1, blocking collectives, shards(): search_handles = lax.all_gather(new_key, 'context', axis=0, tiled=True)  16.9 us
    unnamed x76, local copies, waits for them, and re-layouts  16.9 us
    all_gather x1, blocking collectives, shards(): values = lax.all_gather(cached_value, 'context', axis=0, tiled=True)  16.1 us
    all_gather x1, blocking collectives, shards(): search_handles = lax.all_gather(cached_key, 'context', axis=0, tiled=True)  15.2 us
    all_gather x1, blocking collectives, shards(): lax.all_gather(prefix_state, 'context', axis=2, tiled=True)  14.9 us
    unnamed x1, blocking collectives  8.08 us
    ppermute x3, starting transfers between devices, shards(): lax.ppermute(ring[-1], 'context', [(dev, (dev + 1) % 4) for dev in range(...  6.08 us
  transfers between devices with their start and end apart: 5, of which 0 were waited for; matrix products, arithmetic and copies ran while one was open for 10% of the time, Pallas kernels for 0%

profile of v1, /device:TPU:26, one launch (start us, length us, event | category | flops | bytes accessed | tf_op | source)
XLA Modules:
  0.0 225.6 jit_solution(9443009363479204883)
XLA Ops:
  12.7 1.3 fusion.15
  14.0 78.6 %custom-call.4 = f32[8,1,128,128]{2,3,1,0:T(8,128)S(1)} custom-call(f32[8,1,128,128]{3,2,1,0:T(8,128)S(1)} %fusion.15), custom_call_target="InvertDiagBlocksLowerTriangular" | custom-call | tf_op jit(solution)/shard_map/jit(_solve_triangular)/vmap()/triangular_solve | solution.py:177
  92.7 1.3 compare_and_fusion.3
  94.6 1.0 fusion.22
  95.6 1.7 convolution_convert_fusion
  98.7 1.7 fusion.20
  103.2 1.2 convolution_multiply_fusion.3
  104.4 1.4 fusion.43
  107.1 16.9 %all-gather.2 = bf16[512,1,256]{0,2,1:T(8,128)(2,1)S(1)} all-gather(bf16[128,1,256]{0,2,1:T(8,128)(2,1)S(1)} %pad_maximum_fusion.1), channel_id=4, replica_groups=mesh['group'=2,'context'=4,'head'=4] {'context'}, dimensions={0}, use_global_device_ids=true | all-gather | bytes 327680 | tf_op jit(solution)/shard_map/all_gather | solution.py:266
  125.0 15.2 %all_gather.37 = bf16[8,64,256]{2,1,0:T(8,128)(2,1)} all-gather(bf16[2,64,256]{2,1,0:T(8,128)(2,1)S(1)} %constant_dynamic-slice_fusion.5), channel_id=1, replica_groups=mesh['group'=2,'context'=4,'head'=4] {'context'}, dimensions={0}, use_global_device_ids=true | all-gather | bytes 327680 | tf_op jit(solution)/shard_map/all_gather | solution.py:250
  140.6 16.1 %all_gather.38 = bf16[8,64,256]{2,1,0:T(8,128)(2,1)S(1)} all-gather(bf16[2,64,256]{2,1,0:T(8,128)(2,1)S(1)} %constant_dynamic-slice_fusion.4), channel_id=1, replica_groups=mesh['group'=2,'context'=4,'head'=4] {'context'}, dimensions={0}, use_global_device_ids=true | all-gather | bytes 327680 | tf_op jit(solution)/shard_map/all_gather | solution.py:251
  159.9 1.2 fusion.18
  161.2 2.2 collective-permute-start.1
  166.7 3.6 %collective-permute-start.2 = (bf16[128,256]{1,0:T(8,128)(2,1)}, bf16[128,256]{1,0:T(8,128)(2,1)}, u32[]{:S(2)}, u32[]{:S(2)}) collective-permute-start(bf16[128,256]{1,0:T(8,128)(2,1)} %collective-permute-done.1), channel_id=1, source_target_pairs={{0,4},{4,8},{8,12},{12,0},{1,5},{5,9},{9,13},{13,1},{2,6},{6,10},{... | collective-permute-start | bytes 196616 | tf_op jit(solution)/shard_map/ppermute | solution.py:269
  170.3 14.9 %all_gather.36 = bf16[2,8,128,128]{3,2,0,1:T(8,128)(2,1)S(1)} all-gather(bf16[2,8,32,128]{3,2,0,1:T(8,128)(2,1)S(1)} %copy.150), channel_id=1, replica_groups=mesh['group'=2,'context'=4,'head'=4] {'context'}, dimensions={2}, use_global_device_ids=true | all-gather | bytes 655360 | tf_op jit(solution)/shard_map/all_gather | solution.py:216
  185.2 8.1 %all-reduce = bf16[4]{0:T(256)(128)(2,1)S(1)} all-reduce(bf16[4]{0:T(256)(128)(2,1)S(1)} %dynamic-update-slice), channel_id=1, replica_groups=mesh['group'=2,'context'=4,'head'=4] {'context'}, use_global_device_ids=true, to_apply=%add | all-reduce | flops 4 | bytes 16
  194.2 1.1 copy.152
  196.4 0.9 constant_dynamic-update-slice_fusion.6
  199.9 1.1 fusion.19
  201.0 1.1 copy.165
  203.0 11.3 %while.14 = (s32[]{:T(128)}, f32[8,128,128]{1,2,0:T(8,128)S(1)}, f32[8,128,128]{1,2,0:T(8,128)S(1)}, s32[]{:T(128)}, bf16[4]{0:T(256)(128)(2,1)S(1)}, /*index=5*...) while((s32[]{:T(128)}, f32[8,128,128]{1,2,0:T(8,128)S(1)}, ...), condition=%wide.region_6.7_spmd, body=%wide.region_5.6_spmd.sunk | while | flops 403308544 | bytes 7340196 | solution.py:41
  203.1 1.1 constant_dynamic-slice_fusion.7
  206.8 1.1 constant_dynamic-slice_fusion.7
  210.6 1.1 constant_dynamic-slice_fusion.7
  (182 shorter events, 33.4 us)
Async XLA Ops:
  7.2 99.4 %copy-start = (bf16[128,512]{1,0:T(8,128)(2,1)S(1)}, bf16[128,512]{1,0:T(8,128)(2,1)}, u32[]{:S(2)}) copy-start(bf16[128,512]{1,0:T(8,128)(2,1)} %param.30) | copy-start | bytes 393220
  7.2 195.8 %all-gather.8.cloned.1.call-start = ((), (), s32[]{:S(2)}) async-start(), calls=%async_computation.1 | async-start | bytes 1310720 | tf_op jit(solution)/shard_map/all_gather | solution.py:25
  7.2 3.5 %copy-start.14 = (bf16[128,512]{1,0:T(8,128)(2,1)S(1)}, bf16[128,512]{1,0:T(8,128)(2,1)}, u32[]{:S(2)}) copy-start(bf16[128,512]{1,0:T(8,128)(2,1)} %param.21) | copy-start | bytes 393220
  9.0 1.2 copy-start.24
  11.3 1.0 copy-start.8
  97.4 105.6 %all-gather.6.cloned.1.call-start = ((), (), s32[]{:S(2)}) async-start(), calls=%async_computation | async-start | bytes 1310720 | tf_op jit(solution)/shard_map/all_gather | solution.py:25
  98.2 63.0 %collective-permute-start = (bf16[128,256]{1,0:T(8,128)(2,1)S(1)}, bf16[128,256]{1,0:T(8,128)(2,1)S(1)}, u32[]{:S(2)}, u32[]{:S(2)}) collective-permute-start(bf16[128,256]{1,0:T(8,128)(2,1)S(1)} %constant_dynamic-slice_fusion.2), channel_id=1, source_target_pairs={{0,4},{4,8},{8,12},{12,0},{1,5},{5,9},{9,13},{13,1},{2,6},{6,10},{... | collective-permute-start | bytes 196616 | tf_op jit(solution)/shard_map/ppermute | solution.py:269
  100.4 0.9 copy-start.9
  101.7 0.9 copy-start.15
  124.0 0.9 copy-start.17
  124.9 34.3 %copy-start.5 = (pred[128,512]{1,0:T(8,128)(4,1)}, pred[128,512]{1,0:T(8,128)(4,1)S(1)}, u32[]{:S(2)}) copy-start(pred[128,512]{1,0:T(8,128)(4,1)S(1)} %fusion.50) | copy-start | bytes 196612
  124.9 15.2 %copy-start.26 = (s32[8]{0:T(128)S(1)}, s32[8]{0:T(128)}, u32[]{:S(2)}) copy-start(s32[8]{0:T(128)} %param.37) | copy-start | bytes 100
  124.9 15.6 %copy-start.18 = (bf16[2,64,512]{2,1,0:T(8,128)(2,1)S(1)}, bf16[2,64,512]{2,1,0:T(8,128)(2,1)}, u32[]{:S(2)}) copy-start(bf16[2,64,512]{2,1,0:T(8,128)(2,1)} %param.33) | copy-start | bytes 393220
  140.1 16.5 %copy-start.10 = (bf16[128,1024]{1,0:T(8,128)(2,1)S(1)}, bf16[128,1024]{1,0:T(8,128)(2,1)}, u32[]{:S(2)}) copy-start(bf16[128,1024]{1,0:T(8,128)(2,1)} %param.29) | copy-start | bytes 786436
  156.8 1.0 copy-start.11
  157.8 0.9 copy-start.4
  161.1 3.5 %copy-start.16 = (bf16[2,8,32,128]{3,2,1,0:T(8,128)(2,1)S(1)}, bf16[2,8,32,128]{3,2,1,0:T(8,128)(2,1)}, u32[]{:S(2)}) copy-start(bf16[2,8,32,128]{3,2,1,0:T(8,128)(2,1)} %param.27) | copy-start | bytes 393220
  161.2 3.4 %copy-start.12 = (bf16[128,256]{1,0:T(8,128)(2,1)}, bf16[128,256]{1,0:T(8,128)(2,1)S(1)}, u32[]{:S(2)}) copy-start(bf16[128,256]{1,0:T(8,128)(2,1)S(1)} %collective-permute-done) | copy-start | bytes 196612
  161.2 5.5 %collective-permute-start.1 = (bf16[128,256]{1,0:T(8,128)(2,1)S(1)}, bf16[128,256]{1,0:T(8,128)(2,1)}, u32[]{:S(2)}, u32[]{:S(2)}) collective-permute-start(bf16[128,256]{1,0:T(8,128)(2,1)S(1)} %collective-permute-done), channel_id=1, source_target_pairs={{0,4},{4,8},{8,12},{12,0},{1,5},{5,9},{9,13},{13,1},{2,6},{6,10},{... | collective-permute-start | bytes 196616 | tf_op jit(solution)/shard_map/ppermute | solution.py:269
  166.7 28.8 %collective-permute-start.2 = (bf16[128,256]{1,0:T(8,128)(2,1)}, bf16[128,256]{1,0:T(8,128)(2,1)}, u32[]{:S(2)}, u32[]{:S(2)}) collective-permute-start(bf16[128,256]{1,0:T(8,128)(2,1)} %collective-permute-done.1), channel_id=1, source_target_pairs={{0,4},{4,8},{8,12},{12,0},{1,5},{5,9},{9,13},{13,1},{2,6},{6,10},{... | collective-permute-start | bytes 196616 | tf_op jit(solution)/shard_map/ppermute | solution.py:269
  195.5 1.8 copy-start.13
  196.4 0.9 copy-start.3
  196.4 2.7 %copy-start.28 = (f32[128,4,256]{2,0,1:T(8,128)S(1)}, f32[128,4,256]{2,0,1:T(8,128)}, u32[]{:S(2)}) copy-start(f32[128,4,256]{2,0,1:T(8,128)} %fusion.18) | copy-start | bytes 1572868
  215.0 1.0 copy-start.1
  (10 other events, 7.3 us)
Sparse Core Ops, SparseCore 0:
  97.5 32.0 all-gather.7
  131.7 32.3 all-gather.5
